TPU v7x, 32 devices: a whole 2x2x4 slice. The times are simulated.
32 devices in a mesh: ctx: 8 (over z, x), head: 4 (over y, core).
Axes of the slice: x: 2, y: 2, z: 4, core: 2. Of those that a mesh axis runs over, the one named last changes fastest.
Arguments:
- queries: bfloat16 [4096, 4096], P('ctx', 'head'), may hold values from -5 to 5
- keys: bfloat16 [4096, 512], P('ctx', 'head'), may hold values from -5 to 5
- values: bfloat16 [4096, 512], P('ctx', 'head'), may hold values from -8 to 8
- feature_map: bfloat16 [4, 128, 16], P('head'), may hold values from -0.5 to 0.5
- out_proj: bfloat16 [4096, 8192], P('ctx', 'head'), may hold values from -0.09375 to 0.09375
- teacher: bfloat16 [4096, 8192], P('ctx', 'head'), may hold values from -16 to 16
Outputs:
- student_out: bfloat16 [4096, 8192], P('ctx', 'head')
- loss: float32 [], replicated
- feature_grad: float32 [4, 128, 16], P('head')
All inputs are finite; a program needn't handle non-finite values.
Results may differ from a plain program's by a relative error of at most 0.006.
Values may be sent and summed in bfloat16 or wider, within the bound.
A program may use at most 128 MiB of HBM per device.

v0:
```python
import math
import jax
import jax.numpy as jnp
from jax import lax
from jax.sharding import PartitionSpec as P

D = 8192
HEAD_DIM = 128
GROUP = 8
WIN = 64
exact_mode = lax.Precision.HIGHEST


def shifted(block, axis, distance):
    devices = range(lax.axis_size(axis))
    route = [(i - distance, i) for i in devices if i - distance in devices]
    return lax.ppermute(block, axis, route)


def taylor_square(features):
    feature_count = features.shape[-1]
    outer = features[..., :, None] * features[..., None, :]
    return outer.reshape(features.shape[:-1] + (feature_count * feature_count,))


def square_grad(grad_square, features):
    feature_count = features.shape[-1]
    matrix = grad_square.reshape(features.shape + (feature_count,))
    return jnp.einsum("...fh,...h->...f", matrix, features, precision=exact_mode) + jnp.einsum(
        "...hf,...h->...f", matrix, features, precision=exact_mode
    )


def masked_total(select, member):
    shaped = select.reshape((select.shape[0],) + (1,) * (member.ndim - 1))
    return jnp.sum(jnp.where(shaped, member, jnp.zeros_like(member)), axis=0)


def window_tiles(extended, tok_rows):
    tile_count = tok_rows // WIN
    first = extended[:tok_rows].reshape((tile_count, WIN) + extended.shape[1:])
    second = extended[WIN:].reshape((tile_count, WIN) + extended.shape[1:])
    return jnp.concatenate([first, second], 1)


def local(queries, keys, values, feature_map, out_proj, teacher):
    tok_rows = queries.shape[0]
    kv_groups = keys.shape[1] // HEAD_DIM
    ctx_count = lax.axis_size("ctx")
    ctx_index = lax.axis_index("ctx")
    query_heads = queries.reshape(tok_rows, kv_groups, GROUP, HEAD_DIM)
    key_heads = keys.reshape(tok_rows, kv_groups, HEAD_DIM)
    value_float = values.reshape(tok_rows, kv_groups, HEAD_DIM).astype(jnp.float32)
    query_features = jnp.einsum(
        "tgqe,gef->tgqf", query_heads, feature_map, preferred_element_type=jnp.float32
    )
    key_features = jnp.einsum(
        "tge,gef->tgf", key_heads, feature_map, preferred_element_type=jnp.float32
    )
    rim_rows = shifted(jnp.stack([keys[tok_rows - WIN :], values[tok_rows - WIN :]]), "ctx", 1)
    keys_ext = jnp.concatenate([rim_rows[0], keys], 0).reshape(tok_rows + WIN, kv_groups, HEAD_DIM)
    values_ext = jnp.concatenate([rim_rows[1], values], 0).reshape(
        tok_rows + WIN, kv_groups, HEAD_DIM
    )
    tile_count = tok_rows // WIN
    key_tiles = window_tiles(keys_ext, tok_rows)
    value_tiles = window_tiles(values_ext, tok_rows)
    query_tiles = query_heads.reshape(tile_count, WIN, kv_groups, GROUP, HEAD_DIM)
    scores = jnp.einsum(
        "ntgqe,nsge->ngqts", query_tiles, key_tiles, preferred_element_type=jnp.float32
    ) / math.sqrt(HEAD_DIM)
    tile_pos = lax.broadcasted_iota(jnp.int32, (tile_count, WIN, 2 * WIN), 0)
    query_pos = lax.broadcasted_iota(jnp.int32, (tile_count, WIN, 2 * WIN), 1)
    key_pos = lax.broadcasted_iota(jnp.int32, (tile_count, WIN, 2 * WIN), 2)
    distance = query_pos + WIN - key_pos
    allowed = (
        (distance >= 0)
        & (distance < WIN)
        & (ctx_index * tok_rows + tile_pos * WIN + key_pos - WIN >= 0)
    )
    allowed = allowed[:, None, None]
    scores = jnp.where(allowed, scores, -jnp.inf)
    row_max = jnp.max(scores, axis=-1, keepdims=True)
    weights = jnp.where(allowed, jnp.exp(scores - row_max), 0.0)
    attn_weights = (weights / jnp.sum(weights, axis=-1, keepdims=True)).astype(jnp.bfloat16)
    window_out = jnp.einsum(
        "ngqts,nsge->ntgqe", attn_weights, value_tiles, preferred_element_type=jnp.float32
    ).reshape(tok_rows, kv_groups, GROUP, HEAD_DIM)
    causal = lax.broadcasted_iota(jnp.int32, (tok_rows, tok_rows), 0) >= lax.broadcasted_iota(
        jnp.int32, (tok_rows, tok_rows), 1
    )
    qk_inner = (
        jnp.einsum("tgqf,sgf->gqts", query_features, key_features, precision=exact_mode) / 4.0
    )
    kernel = jnp.where(causal, 1.0 + qk_inner + 0.5 * qk_inner * qk_inner, 0.0)
    numerator = jnp.einsum("gqts,sge->tgqe", kernel, value_float, precision=exact_mode)
    denominator = jnp.transpose(jnp.sum(kernel, axis=-1), (2, 0, 1))
    key_square = taylor_square(key_features)
    own_square_v = jnp.einsum("sgk,sge->gke", key_square, value_float, precision=exact_mode)
    own_linear_v = jnp.einsum("sgf,sge->gfe", key_features, value_float, precision=exact_mode)
    own_values = jnp.sum(value_float, axis=0)
    own_square_k = jnp.sum(key_square, axis=0)
    own_linear_k = jnp.sum(key_features, axis=0)
    own_count = jnp.full((kv_groups,), float(tok_rows), jnp.float32)
    gathered = (
        lax.all_gather(own_square_v[None], "ctx", axis=0, tiled=True),
        lax.all_gather(own_linear_v[None], "ctx", axis=0, tiled=True),
        lax.all_gather(own_values[None], "ctx", axis=0, tiled=True),
        lax.all_gather(own_square_k[None], "ctx", axis=0, tiled=True),
        lax.all_gather(own_linear_k[None], "ctx", axis=0, tiled=True),
        lax.all_gather(own_count[None], "ctx", axis=0, tiled=True),
    )
    lower_select = jnp.arange(ctx_count) < ctx_index
    earlier = tuple((masked_total(lower_select, member) for member in gathered))
    past_square_v, past_linear_v, past_values, past_square_k, past_linear_k, past_count = earlier
    query_square = taylor_square(query_features)
    numerator = (
        numerator
        + jnp.einsum("tgqk,gke->tgqe", query_square, past_square_v, precision=exact_mode) / 32.0
        + jnp.einsum("tgqf,gfe->tgqe", query_features, past_linear_v, precision=exact_mode) / 4.0
        + past_values[None, :, None, :]
    )
    denominator = (
        denominator
        + jnp.einsum("tgqk,gk->tgq", query_square, past_square_k, precision=exact_mode) / 32.0
        + jnp.einsum("tgqf,gf->tgq", query_features, past_linear_k, precision=exact_mode) / 4.0
        + past_count[None, :, None]
    )
    linear_out = numerator / denominator[..., None]
    head_out = (
        (linear_out + window_out)
        .astype(jnp.bfloat16)
        .reshape(tok_rows, kv_groups * GROUP * HEAD_DIM)
    )
    all_heads = lax.all_gather(head_out, "head", axis=1, tiled=True)
    proj_full = lax.all_gather(out_proj, "ctx", axis=0, tiled=True)
    projected = jnp.dot(all_heads, proj_full, preferred_element_type=jnp.float32)
    student_out = projected.astype(jnp.bfloat16)
    residual = student_out.astype(jnp.float32) - teacher.astype(jnp.float32)
    total_rows = tok_rows * ctx_count
    loss_value = lax.psum(jnp.sum(residual * residual), ("ctx", "head")) / (total_rows * D)
    d_student = (2.0 * residual / total_rows).astype(jnp.bfloat16)
    head_terms = lax.dot_general(
        d_student, proj_full, (((1,), (1,)), ((), ())), preferred_element_type=jnp.float32
    )
    head_grad = (
        lax.psum_scatter(head_terms.astype(jnp.bfloat16), "head", scatter_dimension=1, tiled=True)
        .astype(jnp.float32)
        .reshape(tok_rows, kv_groups, GROUP, HEAD_DIM)
    )
    numerator_grad = head_grad / denominator[..., None]
    denominator_grad = -jnp.sum(head_grad * linear_out, axis=-1) / denominator
    kernel_grad = (
        jnp.einsum("tgqe,sge->gqts", numerator_grad, value_float, precision=exact_mode)
        + jnp.transpose(denominator_grad, (1, 2, 0))[..., None]
    )
    inner_grad = jnp.where(causal, kernel_grad * (1.0 + qk_inner), 0.0) / 4.0
    query_grad = jnp.einsum("gqts,sgf->tgqf", inner_grad, key_features, precision=exact_mode)
    key_grad = jnp.einsum("gqts,tgqf->sgf", inner_grad, query_features, precision=exact_mode)
    query_square_grad = (
        jnp.einsum("tgqe,gke->tgqk", numerator_grad, past_square_v, precision=exact_mode)
        + denominator_grad[..., None] * past_square_k[None, :, None, :]
    ) / 32.0
    query_grad = (
        query_grad
        + (
            jnp.einsum("tgqe,gfe->tgqf", numerator_grad, past_linear_v, precision=exact_mode)
            + denominator_grad[..., None] * past_linear_k[None, :, None, :]
        )
        / 4.0
        + square_grad(query_square_grad, query_features)
    )
    own_back_square = jnp.einsum(
        "tgqk,tgqe->gke", query_square, numerator_grad, precision=exact_mode
    )
    own_back_linear = jnp.einsum(
        "tgqf,tgqe->gfe", query_features, numerator_grad, precision=exact_mode
    )
    own_den_square = jnp.einsum(
        "tgqk,tgq->gk", query_square, denominator_grad, precision=exact_mode
    )
    own_den_linear = jnp.einsum(
        "tgqf,tgq->gf", query_features, denominator_grad, precision=exact_mode
    )
    gathered_back = (
        lax.all_gather(own_back_square[None], "ctx", axis=0, tiled=True),
        lax.all_gather(own_back_linear[None], "ctx", axis=0, tiled=True),
        lax.all_gather(own_den_square[None], "ctx", axis=0, tiled=True),
        lax.all_gather(own_den_linear[None], "ctx", axis=0, tiled=True),
    )
    upper_select = jnp.arange(ctx_count) > ctx_index
    later_sums = tuple((masked_total(upper_select, member) for member in gathered_back))
    later_square, later_linear, later_den_square, later_den_linear = later_sums
    key_square_grad = (
        jnp.einsum("gke,sge->sgk", later_square, value_float, precision=exact_mode)
        + later_den_square[None]
    ) / 32.0
    key_grad = (
        key_grad
        + (
            jnp.einsum("gfe,sge->sgf", later_linear, value_float, precision=exact_mode)
            + later_den_linear[None]
        )
        / 4.0
        + square_grad(key_square_grad, key_features)
    )
    own_grad = jnp.einsum(
        "tgqe,tgqf->gef", query_heads.astype(jnp.float32), query_grad, precision=exact_mode
    ) + jnp.einsum("tge,tgf->gef", key_heads.astype(jnp.float32), key_grad, precision=exact_mode)
    feature_grad = lax.psum(own_grad, "ctx")
    return (student_out, loss_value, feature_grad)


def solution(mesh):
    return jax.shard_map(
        local,
        mesh=mesh,
        in_specs=(
            P("ctx", "head"),
            P("ctx", "head"),
            P("ctx", "head"),
            P("head", None, None),
            P("ctx", "head"),
            P("ctx", "head"),
        ),
        out_specs=(P("ctx", "head"), P(), P("head", None, None)),
        check_vma=False,
    )
```

profile of v0, /device:TPU:0, one launch (start us, length us, event | category | flops | bytes accessed | tf_op | source)
XLA Modules:
  0.0 652.8 jit_solution(9237488309166573956)
XLA Ops:
  9.4 5.4 collective-permute-start
  14.8 1.7 fusion.106
  16.7 1.9 fusion.107
  20.9 18.1 %all_gather.39 = f32[8,1,256]{2,1,0:T(1,128)S(1)} all-gather(f32[1,1,256]{2,1,0:T(1,128)S(1)} %broadcast_in_dim.148), channel_id=1, replica_groups=mesh['ctx'=8,'head'=4] {'ctx'}, dimensions={0}, use_global_device_ids=true | all-gather | bytes 9216 | tf_op jit(solution)/shard_map/all_gather | solution.py:109
  40.1 1.9 copy-done.2
  42.0 7.1 %fusion.108 = f32[1,512,8]{0,1,2:T(8,128)S(1)} fusion(f32[256,1,1]{0,1,2:T(1,128)S(1)} %bitcast.398, f32[512,8,256]{0,2,1:T(8,128)S(1)} %bitcast.367), kind=kOutput, calls=%fused_computation.168 | convolution fusion | flops 12582912 | bytes 4211712 | tf_op jit(solution)/shard_map/tgqk,gk->tgq/dot_general | solution.py:125
  49.2 1.2 copy.68
  50.4 1.3 dynamic-slice
  52.3 0.9 dynamic-update-slice
  53.9 18.1 %all-reduce.3 = (f32[128]{0:T(128)S(1)}, f32[8]{0:T(128)}) all-reduce(f32[128]{0:T(128)S(1)} %dynamic-update-slice, f32[8]{0:T(128)S(1)} %dynamic-update-slice.1), channel_id=5, replica_groups=mesh['ctx'=8,'head'=4] {'ctx'}, use_global_device_ids=true, to_apply=%add | all-reduce | flops 136 | bytes 1088
  72.8 3.4 fusion.89
  76.2 1.2 copy.69
  77.4 11.7 %fusion.7 = (f32[8,512]{1,0:T(8,128)S(1)}, f32[512,512,8]{1,0,2:T(8,128)}) fusion(pred[512,512]{0,1:T(8,128)(4,1)} %iota_compare_fusion, f32[512,8,16]{0,2,1:T(8,128)S(1)} %convolution_bitcast_fusion.2, f32[16,512]{1,0:T(8,128)} %copy-done.6), kind=kOutput, calls=%fused_computation.10 | convolution fusion | flops 417329152 | bytes 8962048 | tf_op jit(solution)/shard_map/tgqf,sgf->gqts/dot_general | solution.py:93
  89.8 31.0 %all-gather.1 = f32[128,128]{1,0:T(8,128)S(1)} all-gather(f32[16,128]{1,0:T(8,128)S(1)} %fusion.93), channel_id=3, replica_groups=mesh['ctx'=8,'head'=4] {'ctx'}, dimensions={0}, use_global_device_ids=true | all-gather | bytes 73728 | tf_op jit(solution)/shard_map/all_gather | solution.py:107
  120.9 3.2 fusion.80
  124.1 9.7 %fusion.5 = f32[8,512,128]{1,2,0:T(8,128)} fusion(f32[512,512,8]{1,0,2:T(8,128)} %get-tuple-element.13, pred[512,512]{0,1:T(8,128)(4,1)S(1)} %copy-done.17, bf16[512,128]{1,0:T(8,128)(2,1)S(1)} %copy-done.5), kind=kOutput, calls=%fused_computation.7 | convolution fusion | flops 3233808384 | bytes 10878976 | tf_op jit(solution)/shard_map/gqts,sge->tgqe/dot_general | solution.py:96
  133.9 1.3 fusion.76
  135.2 18.2 %all-gather.8 = f32[8,1,128]{2,1,0:T(1,128)S(1)} all-gather(f32[1,1,128]{2,1,0:T(1,128)S(1)} %bitcast.399), channel_id=4, replica_groups=mesh['ctx'=8,'head'=4] {'ctx'}, dimensions={0}, use_global_device_ids=true | all-gather | bytes 4608 | tf_op jit(solution)/shard_map/all_gather | solution.py:108
  155.9 1.3 fusion.27
  157.3 2.6 convolution_bitcast_fusion
  159.9 1.2 copy.52
  161.1 1.8 copy.53
  162.9 1.4 select_reduce_fusion.1
  164.3 8.5 %add_convert_fusion = (bf16[512,1,8,128]{0,3,2,1:T(8,128)(2,1)}, f32[512,1,8,128]{0,3,2,1:T(8,128)}) fusion(f32[512,1,8,128]{0,3,2,1:T(8,128)} %copy.53, f32[512,8]{0,1:T(8,128)} %bitcast.390, f32[128]{0:T(128)S(1)} %copy-done.26, f32[128,512,8]{1,0,2:T(8,128)} %fusion.80, f32[512,8,256]{0,2,1:T(8,128)} %bitcast.368, ...), kind=kOutput, calls=%fused_computation.38 | convolution fusion | flops 1614807040 | bytes 13779456 | tf_op jit(solution)/shard_map/tgqk,gke->tgqe/dot_general | solution.py:119
  173.8 30.9 %all-gather.15.cloned.1.call-done = bf16[512,4096]{0,1:T(8,128)(2,1)} async-done(((bf16[512,1024]{0,1:T(8,128)(2,1)}), bf16[512,4096]{0,1:T(8,128)(2,1)}) %all-gather.15.cloned.1.call-update) | async-done | bytes 4194320 | tf_op jit(solution)/shard_map/all_gather | solution.py:135
  204.8 229.8 %all-gather.17.cloned.1.call-done = bf16[4096,2048]{1,0:T(8,128)(2,1)} async-done(((bf16[512,2048]{1,0:T(8,128)(2,1)}), bf16[4096,2048]{1,0:T(8,128)(2,1)}) %all-gather.17.cloned.1.call-update) | async-done | bytes 16777232 | tf_op jit(solution)/shard_map/all_gather | solution.py:136
  434.6 14.8 %multiply_reduce_fusion.2 = (f32[]{:T(128)}, bf16[512,2048]{1,0:T(8,128)(2,1)S(1)}) fusion(bf16[512,2048]{1,0:T(8,128)(2,1)S(1)} %copy-done.28, bf16[512,4096]{0,1:T(8,128)(2,1)} %all-gather.15.cloned.1.call-done, bf16[4096,2048]{1,0:T(8,128)(2,1)} %all-gather.17.cloned.1.call-done), kind=kOutput, calls=%fused_computation.16 | convolution fusion | flops 8596226048 | bytes 25165828 | tf_op jit(solution)/shard_map/dot_general | solution.py:137
  449.3 1.3 copy-done.29
  450.7 13.8 %convolution_convert_fusion = bf16[512,4096]{1,0:T(8,128)(2,1)} fusion(bf16[4096,2048]{1,0:T(8,128)(2,1)} %all-gather.17.cloned.1.call-done, bf16[512,2048]{1,0:T(8,128)(2,1)S(1)} %copy-done.28, bf16[512,2048]{1,0:T(8,128)(2,1)S(1)} %get-tuple-element.21), kind=kOutput, calls=%fused_computation.9 | convolution fusion | flops 8597274624 | bytes 25165824 | tf_op jit(solution)/shard_map/dot_general | solution.py:143
  465.1 0.8 copy.98
  466.0 39.3 %psum.14 = f32[]{:T(128)} all-reduce(f32[]{:T(128)} %get-tuple-element.20), channel_id=1, replica_groups=mesh['ctx'=8,'head'=4] {'ctx','head'}, use_global_device_ids=true, to_apply=%region_13.14 | all-reduce | flops 1 | bytes 8 | tf_op jit(solution)/shard_map/psum | solution.py:141
  505.9 2.1 reduce-scatter.2.cloned.1.call-done
  508.0 1.5 copy.57
  509.5 2.3 multiply_reduce_fusion.3
  512.3 3.3 convolution_bitcast_fusion.7
  516.1 4.3 convolution_bitcast_fusion.3
  520.4 20.5 %all-gather.9 = f32[8,1,256]{2,1,0:T(1,128)S(1)} all-gather(f32[1,1,256]{2,1,0:T(1,128)S(1)} %convolution_bitcast_fusion.7), channel_id=9, replica_groups=mesh['ctx'=8,'head'=4] {'ctx'}, dimensions={0}, use_global_device_ids=true | all-gather | bytes 9216 | tf_op jit(solution)/shard_map/all_gather | solution.py:188
  540.9 1.5 convolution_bitcast_fusion.6
  542.4 30.8 %all-gather.4 = f32[128,128]{1,0:T(8,128)S(1)} all-gather(f32[16,128]{1,0:T(8,128)S(1)} %convolution_bitcast_fusion.6), channel_id=6, replica_groups=mesh['ctx'=8,'head'=4] {'ctx'}, dimensions={0}, use_global_device_ids=true | all-gather | bytes 73728 | tf_op jit(solution)/shard_map/all_gather | solution.py:187
  573.6 17.3 %all-reduce.2 = f32[128]{0:T(128)S(1)} all-reduce(f32[128]{0:T(128)S(1)} %dynamic-update-slice.2), channel_id=7, replica_groups=mesh['ctx'=8,'head'=4] {'ctx'}, use_global_device_ids=true, to_apply=%add.2 | all-reduce | flops 128 | bytes 1024
  591.7 4.1 fusion.9
  596.6 1.1 multiply_reduce_fusion.1
  597.8 2.2 fusion.38
  600.0 10.8 %fusion.3 = f32[8,512,512]{1,2,0:T(8,128)S(1)} fusion(f32[512,512,8]{1,0,2:T(8,128)S(1)} %bitcast.401, f32[8,512]{1,0:T(8,128)S(1)} %get-tuple-element.7, pred[512,512]{0,1:T(8,128)(4,1)S(1)} %copy-done.18, bf16[512,128]{1,0:T(8,128)(2,1)S(1)} %copy-done.5, f32[64,8,8,128]{3,2,1,0:T(8,128)S(1)} %bitcast.380, bf16[512,1024]{1,0:T(8,128)(2,1)S(1)} %copy-done.10), kind=kOutput, calls=%fused_computation.4 | convolution fusion | flops 3234856960 | bytes 20332544 | tf_op jit(solution)/shard_map/tgqe,sge->gqts/dot_general | solution.py:154
  610.8 4.0 fusion.31
  615.5 7.1 %convolution_bitcast_fusion.4 = f32[512,1,16]{0,2,1:T(8,128)S(1)} fusion(f32[512,8,16]{0,2,1:T(8,128)S(1)} %convolution_bitcast_fusion.2, f32[8,512,512]{1,2,0:T(8,128)S(1)} %fusion.3), kind=kOutput, calls=%fused_computation.65 | convolution fusion | flops 402653184 | bytes 8683520 | tf_op jit(solution)/shard_map/gqts,tgqf->sgf/dot_general | solution.py:159
  622.6 1.4 select_reduce_fusion
  624.9 20.0 %psum.15 = f32[1,128,16]{1,2,0:T(8,128)} all-reduce(f32[1,128,16]{1,2,0:T(8,128)S(1)} %fusion.46), channel_id=1, replica_groups=mesh['ctx'=8,'head'=4] {'ctx'}, use_global_device_ids=true, to_apply=%region_20.21 | all-reduce | flops 2048 | bytes 16384 | tf_op jit(solution)/shard_map/psum | solution.py:210
  (122 shorter events, 16.7 us)
Async XLA Ops:
  7.2 7.7 %copy-start = (bf16[1,128,16]{1,2,0:T(8,128)(2,1)S(1)}, bf16[1,128,16]{1,2,0:T(8,128)(2,1)}, u32[]{:S(2)}) copy-start(bf16[1,128,16]{1,2,0:T(8,128)(2,1)} %param.9) | copy-start | bytes 12292
  7.2 12.8 %copy-start.5 = (bf16[512,128]{1,0:T(8,128)(2,1)S(1)}, bf16[512,128]{1,0:T(8,128)(2,1)}, u32[]{:S(2)}) copy-start(bf16[512,128]{1,0:T(8,128)(2,1)} %param.8) | copy-start | bytes 393220
  7.2 31.8 %copy-start.4 = (bf16[512,1024]{1,0:T(8,128)(2,1)S(1)}, bf16[512,1024]{1,0:T(8,128)(2,1)}, u32[]{:S(2)}) copy-start(bf16[512,1024]{1,0:T(8,128)(2,1)} %param.6) | copy-start | bytes 3145732
  7.2 155.7 %all-gather.19.cloned.1.call-start = ((), (), s32[]{:S(2)}) async-start(), calls=%async_computation.4 | async-start | bytes 1179648 | tf_op jit(solution)/shard_map/all_gather | solution.py:106
  9.4 145.0 %collective-permute-start = (bf16[2,64,128]{2,1,0:T(8,128)(2,1)}, bf16[2,64,128]{2,1,0:T(8,128)(2,1)}, u32[]{:S(2)}, u32[]{:S(2)}) collective-permute-start(bf16[2,64,128]{2,1,0:T(8,128)(2,1)} %pad_maximum_fusion.2), channel_id=1, source_target_pairs={{0,4},{4,8},{8,12},{12,16},{16,20},{20,24},{24,28},{1,5},{5,9},{9,... | collective-permute-start | bytes 98312 | tf_op jit(solution)/shard_map/ppermute | solution.py:17
  16.6 4.3 copy-start.6
  18.7 186.1 %all-gather.15.cloned.1.call-start = ((), (), s32[]{:S(2)}) async-start(), calls=%async_computation.1 | async-start | bytes 5242880 | tf_op jit(solution)/shard_map/all_gather | solution.py:135
  40.0 2.0 copy-start.2
  40.1 9.0 %copy-start.21 = (f32[256]{0:T(256)}, f32[256]{0:T(256)S(1)}, u32[]{:S(2)}) copy-start(f32[256]{0:T(256)S(1)} %fusion.82) | copy-start | bytes 3076
  72.2 0.6 copy-start.23
  77.4 11.7 %copy-start.30 = (f32[8]{0:T(128)S(1)}, f32[8]{0:T(128)}, u32[]{:S(2)}) copy-start(f32[8]{0:T(128)} %get-tuple-element.4) | copy-start | bytes 100
  89.2 34.9 %copy-start.17 = (pred[512,512]{0,1:T(8,128)(4,1)S(1)}, pred[512,512]{0,1:T(8,128)(4,1)}, u32[]{:S(2)}) copy-start(pred[512,512]{0,1:T(8,128)(4,1)} %iota_compare_fusion) | copy-start | bytes 786436
  124.1 9.8 %copy-start.19 = (f32[1,512,8]{1,2,0:T(8,128)S(1)}, f32[1,512,8]{1,2,0:T(8,128)}, u32[]{:S(2)}) copy-start(f32[1,512,8]{1,2,0:T(8,128)} %copy.68) | copy-start | bytes 49156
  124.1 9.8 %copy-start.20 = (f32[1,512,8]{1,2,0:T(8,128)S(1)}, f32[1,512,8]{1,2,0:T(8,128)}, u32[]{:S(2)}) copy-start(f32[1,512,8]{1,2,0:T(8,128)} %copy.69) | copy-start | bytes 49156
  124.1 11.1 %copy-start.25 = (f32[128]{0:T(128)S(1)}, f32[128]{0:T(128)}, u32[]{:S(2)}) copy-start(f32[128]{0:T(128)} %convert_reduce_fusion) | copy-start | bytes 1540
  124.1 29.3 %copy-start.27 = (s32[64]{0:T(128)S(1)}, s32[64]{0:T(128)}, u32[]{:S(2)}) copy-start(s32[64]{0:T(128)} %iota_add_fusion) | copy-start | bytes 772
  133.9 21.3 %copy-start.8 = (bf16[512,128]{1,0:T(8,128)(2,1)S(1)}, bf16[512,128]{1,0:T(8,128)(2,1)}, u32[]{:S(2)}) copy-start(bf16[512,128]{1,0:T(8,128)(2,1)} %param.7) | copy-start | bytes 393220
  161.1 3.2 copy-start.26
  164.3 8.5 %copy-start.12 = (f32[256,128]{1,0:T(8,128)}, f32[256,128]{1,0:T(8,128)S(1)}, u32[]{:S(2)}) copy-start(f32[256,128]{1,0:T(8,128)S(1)} %select_reduce_fusion.1) | copy-start | bytes 393220
  172.8 261.8 %copy-start.28 = (bf16[512,2048]{1,0:T(8,128)(2,1)S(1)}, bf16[512,2048]{1,0:T(8,128)(2,1)}, u32[]{:S(2)}) copy-start(bf16[512,2048]{1,0:T(8,128)(2,1)} %param.11) | copy-start | bytes 6291460
  172.8 261.7 %all-gather.17.cloned.1.call-start = ((), (), s32[]{:S(2)}) async-start(), calls=%async_computation.2 | async-start | bytes 18874368 | tf_op jit(solution)/shard_map/all_gather | solution.py:136
  173.6 334.4 %reduce-scatter.2.cloned.1.call-start = ((), (), s32[]{:S(2)}) async-start(), calls=%async_computation.3 | async-start | bytes 5242880 | tf_op jit(solution)/shard_map/reduce_scatter | solution.py:147
  449.3 1.3 copy-start.29
  464.4 0.7 copy-start.14
  464.5 158.1 %all-gather.21.cloned.1.call-start = ((), (), s32[]{:S(2)}) async-start(), calls=%async_computation.5 | async-start | bytes 1179648 | tf_op jit(solution)/shard_map/all_gather | solution.py:186
  509.5 2.3 copy-start.15
  509.5 2.8 copy-start.3
  512.3 3.8 copy-start.10
  516.1 24.8 %copy-start.16 = (f32[512,1,8]{0,2,1:T(8,128)S(1)}, f32[512,1,8]{0,2,1:T(8,128)}, u32[]{:S(2)}) copy-start(f32[512,1,8]{0,2,1:T(8,128)} %fusion.76) | copy-start | bytes 49156
  540.9 50.2 %copy-start.11 = (f32[512,8]{1,0:T(8,128)S(1)}, f32[512,8]{1,0:T(8,128)}, u32[]{:S(2)}) copy-start(f32[512,8]{1,0:T(8,128)} %copy.98) | copy-start | bytes 49156
  542.4 49.3 %copy-start.13 = (f32[256,128]{1,0:T(8,128)S(1)}, f32[256,128]{1,0:T(8,128)}, u32[]{:S(2)}) copy-start(f32[256,128]{1,0:T(8,128)} %copy-done.12) | copy-start | bytes 393220
  542.4 49.3 %copy-start.22 = (f32[256]{0:T(256)S(1)}, f32[256]{0:T(256)}, u32[]{:S(2)}) copy-start(f32[256]{0:T(256)} %copy-done.21) | copy-start | bytes 3076
  595.8 4.1 slice-start
  596.6 1.1 copy-start.24
  596.6 3.4 slice-start.1
  597.8 2.2 copy-start.18
  600.0 10.8 %copy-start.7 = (f32[16,512]{1,0:T(8,128)S(1)}, f32[16,512]{1,0:T(8,128)}, u32[]{:S(2)}) copy-start(f32[16,512]{1,0:T(8,128)} %copy-done.6) | copy-start | bytes 98308
  615.5 29.4 %copy-start.1 = (bf16[1,128,16]{1,2,0:T(8,128)(2,1)S(1)}, bf16[1,128,16]{1,2,0:T(8,128)(2,1)}, u32[]{:S(2)}) copy-start(bf16[1,128,16]{1,2,0:T(8,128)(2,1)} %param.9) | copy-start | bytes 12292
  622.6 2.2 copy-start.9
Sparse Core Ops, SparseCore 0:
  18.8 40.0 all-gather.18
  173.0 31.7 all-gather.14
  206.9 227.6 all-gather.16
  464.6 43.3 reduce-scatter.1
  520.5 40.2 all-gather.20
where the time goes:
time: 660 us; the launch traced here: 653 us
  waiting for transfers between devices  264 us (40%)
  blocking collectives  213 us (32%)
  matrix products  119 us (18%)
  local copies, waits for them, and re-layouts  19.3 us (3%)
  between operations  16.9 us (3%)
  other arithmetic  14.9 us (2%)
    all_gather x1, waiting for transfers between devices, local(): proj_full = lax.all_gather(out_proj, 'ctx', axis=0, tiled=True)  230 us
    psum x1, blocking collectives, local(): lax.psum(jnp.sum(residual * residual), ('ctx', 'head')) / (total_rows * D)  39.3 us
    unnamed x2, blocking collectives  35.4 us
    all_gather x1, blocking collectives, local(): lax.all_gather(own_linear_v[None], 'ctx', axis=0, tiled=True)  31 us
    all_gather x1, waiting for transfers between devices, local(): all_heads = lax.all_gather(head_out, 'head', axis=1, tiled=True)  30.9 us
    all_gather x1, blocking collectives, local(): lax.all_gather(own_back_linear[None], 'ctx', axis=0, tiled=True)  30.8 us
    all_gather x1, blocking collectives, local(): lax.all_gather(own_den_square[None], 'ctx', axis=0, tiled=True)  20.5 us
    psum x1, blocking collectives, local(): feature_grad = lax.psum(own_grad, 'ctx')  20 us
  transfers between devices with their start and end apart: 6, of which 3 were waited for; matrix products, arithmetic and copies ran while one was open for 14% of the time, Pallas kernels for 0%

commit v1 on v0

--- a/solution.py
+++ b/solution.py
@@ -132,7 +132,20 @@
         .astype(jnp.bfloat16)
         .reshape(tok_rows, kv_groups * GROUP * HEAD_DIM)
     )
-    all_heads = lax.all_gather(head_out, "head", axis=1, tiled=True)
+
+    def store_bands_for(my_tile):
+        named_axis = "head"
+        extent = jax.lax.psum(1, named_axis)
+        new = [None] * extent
+        by_rank = [(k, (k + 1) % extent) for k in range(extent)]
+        new[extent - 1] = my_tile
+        for q in range(extent - 2, -1, -1):
+            new[q] = jax.lax.ppermute(new[q + 1], named_axis, by_rank)
+        return jnp.roll(
+            jnp.concatenate(new, 1), (jax.lax.axis_index(named_axis) + 1) * my_tile.shape[1], 1
+        )
+
+    all_heads = store_bands_for(head_out)
     proj_full = lax.all_gather(out_proj, "ctx", axis=0, tiled=True)
     projected = jnp.dot(all_heads, proj_full, preferred_element_type=jnp.float32)
     student_out = projected.astype(jnp.bfloat16)

time: 660 us -> 510 us (0.77)
  waiting for transfers between devices: 264 us -> 106 us
  local copies, waits for them, and re-layouts: 19.3 us -> 31.1 us
    all_gather x1, waiting for transfers between devices: 230 us -> 60.6 us  [local(): proj_full = lax.all_gather(out_proj, 'ctx', axis=0, tiled=True)]
    ppermute x0 -> x3, waiting for transfers between devices: none -> 43.1 us  [store_bands_for(): new[q] = jax.lax.ppermute(new[q + 1], named_axis, by_rank)]
    all_gather x1 -> x0, waiting for transfers between devices: 30.9 us -> none  [local(): all_heads = lax.all_gather(head_out, 'head', axis=1, tiled=True)]
    unnamed x75 -> x82, local copies, waits for them, and re-layouts: 9.29 us -> 20.1 us
  transfers between devices with their start and end apart: 6 -> 8, of which waited for: 3 -> 5; matrix products, arithmetic and copies ran while one was open for 14% -> 21% of each run, Pallas kernels for 0% -> 0%
where the time goes in v1:
time: 510 us; the launch traced here: 502 us
  blocking collectives  214 us (42%)
  matrix products  114 us (22%)
  waiting for transfers between devices  106 us (21%)
  local copies, waits for them, and re-layouts  31.1 us (6%)
  between operations  17 us (3%)
  other arithmetic  15 us (3%)
  starting transfers between devices  5.6 us (1%)
    all_gather x1, waiting for transfers between devices, local(): proj_full = lax.all_gather(out_proj, 'ctx', axis=0, tiled=True)  60.6 us
    ppermute x3, waiting for transfers between devices, store_bands_for(): new[q] = jax.lax.ppermute(new[q + 1], named_axis, by_rank)  43.1 us
    psum x1, blocking collectives, local(): lax.psum(jnp.sum(residual * residual), ('ctx', 'head')) / (total_rows * D)  39.3 us
    unnamed x2, blocking collectives  35.7 us
    all_gather x1, blocking collectives, local(): lax.all_gather(own_linear_v[None], 'ctx', axis=0, tiled=True)  31.1 us
    all_gather x1, blocking collectives, local(): lax.all_gather(own_back_linear[None], 'ctx', axis=0, tiled=True)  30.7 us
    all_gather x1, blocking collectives, local(): lax.all_gather(own_den_square[None], 'ctx', axis=0, tiled=True)  20.6 us
    unnamed x82, local copies, waits for them, and re-layouts  20.1 us
  transfers between devices with their start and end apart: 8, of which 5 were waited for; matrix products, arithmetic and copies ran while one was open for 21% of the time, Pallas kernels for 0%

profile of v1, /device:TPU:0, one launch (start us, length us, event | category | flops | bytes accessed | tf_op | source)
XLA Modules:
  0.0 502.2 jit_solution(14417146907601765747)
XLA Ops:
  9.2 1.9 fusion.113
  14.0 5.4 %collective-permute-start = (bf16[2,64,128]{2,1,0:T(8,128)(2,1)}, bf16[2,64,128]{2,1,0:T(8,128)(2,1)}, u32[]{:S(2)}, u32[]{:S(2)}) collective-permute-start(bf16[2,64,128]{2,1,0:T(8,128)(2,1)} %pad_maximum_fusion.2), channel_id=1, source_target_pairs={{0,4},{4,8},{8,12},{12,16},{16,20},{20,24},{24,28},{1,5},{5,9},{9,... | collective-permute-start | bytes 98312 | tf_op jit(solution)/shard_map/ppermute | solution.py:17
  19.5 18.1 %all_gather.36 = f32[8,1,256]{2,1,0:T(1,128)S(1)} all-gather(f32[1,1,256]{2,1,0:T(1,128)S(1)} %broadcast_in_dim.148), channel_id=1, replica_groups=mesh['ctx'=8,'head'=4] {'ctx'}, dimensions={0}, use_global_device_ids=true | all-gather | bytes 9216 | tf_op jit(solution)/shard_map/all_gather | solution.py:109
  38.7 2.0 copy-done.2
  40.8 7.1 %fusion.114 = f32[1,512,8]{0,1,2:T(8,128)S(1)} fusion(f32[256,1,1]{0,1,2:T(1,128)S(1)} %bitcast.399, f32[512,8,256]{0,2,1:T(8,128)S(1)} %bitcast.366), kind=kOutput, calls=%fused_computation.179 | convolution fusion | flops 12582912 | bytes 4211712 | tf_op jit(solution)/shard_map/tgqk,gk->tgq/dot_general | solution.py:125
  47.9 1.2 copy.68
  51.4 18.4 %all-reduce.3 = (f32[128]{0:T(128)S(1)}, f32[8]{0:T(128)}) all-reduce(f32[128]{0:T(128)S(1)} %dynamic-update-slice, f32[8]{0:T(128)S(1)} %dynamic-update-slice.1), channel_id=5, replica_groups=mesh['ctx'=8,'head'=4] {'ctx'}, use_global_device_ids=true, to_apply=%add | all-reduce | flops 136 | bytes 1088
  70.0 3.4 fusion.94
  74.7 18.1 %all-gather.8 = f32[8,1,128]{2,1,0:T(1,128)S(1)} all-gather(f32[1,1,128]{2,1,0:T(1,128)S(1)} %bitcast.400), channel_id=4, replica_groups=mesh['ctx'=8,'head'=4] {'ctx'}, dimensions={0}, use_global_device_ids=true | all-gather | bytes 4608 | tf_op jit(solution)/shard_map/all_gather | solution.py:108
  93.8 31.1 %all-gather.1 = f32[128,128]{1,0:T(8,128)S(1)} all-gather(f32[16,128]{1,0:T(8,128)S(1)} %fusion.99), channel_id=3, replica_groups=mesh['ctx'=8,'head'=4] {'ctx'}, dimensions={0}, use_global_device_ids=true | all-gather | bytes 73728 | tf_op jit(solution)/shard_map/all_gather | solution.py:107
  124.9 1.3 fusion.93
  126.4 9.4 %fusion.7 = (f32[8,512]{1,0:T(8,128)S(1)}, f32[512,512,8]{1,0,2:T(8,128)S(1)}) fusion(pred[512,512]{0,1:T(8,128)(4,1)S(1)} %iota_compare_fusion, f32[512,8,16]{0,2,1:T(8,128)S(1)} %convolution_bitcast_fusion.2, f32[16,512]{1,0:T(8,128)} %copy-done.6), kind=kOutput, calls=%fused_computation.10 | convolution fusion | flops 417329152 | bytes 8962048 | tf_op jit(solution)/shard_map/tgqf,sgf->gqts/dot_general | solution.py:93
  135.9 1.8 fusion.81
  137.8 3.1 fusion.85
  141.0 6.2 %fusion.5 = f32[8,512,128]{1,2,0:T(8,128)} fusion(f32[512,512,8]{1,0,2:T(8,128)S(1)} %get-tuple-element.13, pred[512,512]{0,1:T(8,128)(4,1)S(1)} %iota_compare_fusion, bf16[512,128]{1,0:T(8,128)(2,1)S(1)} %copy-done.5), kind=kOutput, calls=%fused_computation.7 | convolution fusion | flops 3233808384 | bytes 10878976 | tf_op jit(solution)/shard_map/gqts,sge->tgqe/dot_general | solution.py:96
  149.6 1.3 fusion.32
  151.0 2.6 convolution_bitcast_fusion
  154.8 1.8 copy.53
  156.6 1.4 select_reduce_fusion.1
  158.0 8.3 %add_convert_fusion = (bf16[512,1,8,128]{0,3,2,1:T(8,128)(2,1)S(1)}, f32[512,1,8,128]{0,3,2,1:T(8,128)}) fusion(f32[512,1,8,128]{0,3,2,1:T(8,128)} %copy.53, f32[512,8]{0,1:T(8,128)} %bitcast.391, f32[128]{0:T(128)S(1)} %copy-done.26, f32[128,512,8]{1,0,2:T(8,128)} %fusion.85, f32[512,8,256]{0,2,1:T(8,128)} %bitcast.367, ...), kind=kOutput, calls=%fused_computation.40 | convolution fusion | flops 1614807040 | bytes 13779456 | tf_op jit(solution)/shard_map/tgqk,gke->tgqe/dot_general | solution.py:119
  166.3 14.2 %collective-permute-done.1 = bf16[512,1024]{0,1:T(8,128)(2,1)S(1)} collective-permute-done((bf16[512,1024]{0,1:T(8,128)(2,1)S(1)}, bf16[512,1024]{0,1:T(8,128)(2,1)S(1)}, u32[]{:S(2)}, u32[]{:S(2)}) %collective-permute-start.1) | collective-permute-done | bytes 1048608 | tf_op jit(solution)/shard_map/ppermute | solution.py:143
  180.5 14.3 %collective-permute-done.2 = bf16[512,1024]{0,1:T(8,128)(2,1)} collective-permute-done((bf16[512,1024]{0,1:T(8,128)(2,1)S(1)}, bf16[512,1024]{0,1:T(8,128)(2,1)}, u32[]{:S(2)}, u32[]{:S(2)}) %collective-permute-start.2) | collective-permute-done | bytes 1048608 | tf_op jit(solution)/shard_map/ppermute | solution.py:143
  194.8 14.5 %collective-permute-done.3 = bf16[512,1024]{0,1:T(8,128)(2,1)} collective-permute-done((bf16[512,1024]{0,1:T(8,128)(2,1)}, bf16[512,1024]{0,1:T(8,128)(2,1)}, u32[]{:S(2)}, u32[]{:S(2)}) %collective-permute-start.3) | collective-permute-done | bytes 1048608 | tf_op jit(solution)/shard_map/ppermute | solution.py:143
  209.4 2.4 constant_dynamic-update-slice_fusion.7
  211.7 2.3 constant_dynamic-update-slice_fusion.6
  216.1 2.3 constant_dynamic-update-slice_fusion.3
  218.4 2.3 constant_dynamic-update-slice_fusion.2
  222.8 60.6 %all-gather.14.cloned.1.call-done = bf16[4096,2048]{1,0:T(8,128)(2,1)} async-done(((bf16[512,2048]{1,0:T(8,128)(2,1)}), bf16[4096,2048]{1,0:T(8,128)(2,1)}) %all-gather.14.cloned.1.call-update) | async-done | bytes 16777232 | tf_op jit(solution)/shard_map/all_gather | solution.py:149
  283.3 15.3 %multiply_reduce_fusion.2 = (f32[]{:T(128)}, bf16[512,2048]{1,0:T(8,128)(2,1)S(1)}) fusion(bf16[512,2048]{1,0:T(8,128)(2,1)} %param.11, bf16[4096,2048]{1,0:T(8,128)(2,1)} %all-gather.14.cloned.1.call-done, bf16[512,8192]{0,1:T(8,128)(2,1)} %constant_dynamic-update-slice_fusion, s32[]{:T(128)S(6)} %select_n.73), kind=kOutput, calls=%fused_computation.16 | convolution fusion | flops 8596226048 | bytes 25165832 | tf_op jit(solution)/shard_map/dot_general | solution.py:150
  298.6 1.3 copy-done.28
  299.9 13.8 %convolution_convert_fusion = bf16[512,4096]{1,0:T(8,128)(2,1)} fusion(bf16[4096,2048]{1,0:T(8,128)(2,1)} %all-gather.14.cloned.1.call-done, bf16[512,2048]{1,0:T(8,128)(2,1)S(1)} %copy-done.27, bf16[512,2048]{1,0:T(8,128)(2,1)S(1)} %get-tuple-element.21), kind=kOutput, calls=%fused_computation.9 | convolution fusion | flops 8597274624 | bytes 25165824 | tf_op jit(solution)/shard_map/dot_general | solution.py:156
  315.3 39.3 %psum.14 = f32[]{:T(128)} all-reduce(f32[]{:T(128)} %get-tuple-element.20), channel_id=1, replica_groups=mesh['ctx'=8,'head'=4] {'ctx','head'}, use_global_device_ids=true, to_apply=%region_13.14 | all-reduce | flops 1 | bytes 8 | tf_op jit(solution)/shard_map/psum | solution.py:154
  355.3 2.1 reduce-scatter.2.cloned.1.call-done
  357.3 1.5 copy.57
  358.8 2.3 multiply_reduce_fusion.3
  361.8 3.3 convolution_bitcast_fusion.7
  365.6 4.2 convolution_bitcast_fusion.3
  369.9 20.6 %all-gather.9 = f32[8,1,256]{2,1,0:T(1,128)S(1)} all-gather(f32[1,1,256]{2,1,0:T(1,128)S(1)} %convolution_bitcast_fusion.7), channel_id=9, replica_groups=mesh['ctx'=8,'head'=4] {'ctx'}, dimensions={0}, use_global_device_ids=true | all-gather | bytes 9216 | tf_op jit(solution)/shard_map/all_gather | solution.py:201
  390.6 1.5 convolution_bitcast_fusion.6
  392.0 30.7 %all-gather.4 = f32[128,128]{1,0:T(8,128)S(1)} all-gather(f32[16,128]{1,0:T(8,128)S(1)} %convolution_bitcast_fusion.6), channel_id=6, replica_groups=mesh['ctx'=8,'head'=4] {'ctx'}, dimensions={0}, use_global_device_ids=true | all-gather | bytes 73728 | tf_op jit(solution)/shard_map/all_gather | solution.py:200
  423.1 17.3 %all-reduce.2 = f32[128]{0:T(128)S(1)} all-reduce(f32[128]{0:T(128)S(1)} %dynamic-update-slice.2), channel_id=7, replica_groups=mesh['ctx'=8,'head'=4] {'ctx'}, use_global_device_ids=true, to_apply=%add.2 | all-reduce | flops 128 | bytes 1024
  441.2 4.1 fusion.9
  447.3 2.2 fusion.43
  449.5 10.8 %fusion.3 = f32[8,512,512]{1,2,0:T(8,128)S(1)} fusion(f32[512,512,8]{1,0,2:T(8,128)S(1)} %bitcast.402, f32[8,512]{1,0:T(8,128)S(1)} %get-tuple-element.7, pred[512,512]{0,1:T(8,128)(4,1)S(1)} %copy-done.19, bf16[512,128]{1,0:T(8,128)(2,1)S(1)} %copy-done.5, f32[64,8,8,128]{3,2,1,0:T(8,128)S(1)} %bitcast.381, bf16[512,1024]{1,0:T(8,128)(2,1)S(1)} %copy-done.11), kind=kOutput, calls=%fused_computation.4 | convolution fusion | flops 3234856960 | bytes 20332544 | tf_op jit(solution)/shard_map/tgqe,sge->gqts/dot_general | solution.py:167
  460.3 4.0 fusion.36
  465.0 7.1 %convolution_bitcast_fusion.4 = f32[512,1,16]{0,2,1:T(8,128)S(1)} fusion(f32[512,8,16]{0,2,1:T(8,128)S(1)} %convolution_bitcast_fusion.2, f32[8,512,512]{1,2,0:T(8,128)S(1)} %fusion.3), kind=kOutput, calls=%fused_computation.67 | convolution fusion | flops 402653184 | bytes 8683520 | tf_op jit(solution)/shard_map/gqts,tgqf->sgf/dot_general | solution.py:172
  472.0 1.4 select_reduce_fusion
  474.4 20.0 %psum.15 = f32[1,128,16]{1,2,0:T(8,128)} all-reduce(f32[1,128,16]{1,2,0:T(8,128)S(1)} %fusion.51), channel_id=1, replica_groups=mesh['ctx'=8,'head'=4] {'ctx'}, use_global_device_ids=true, to_apply=%region_20.21 | all-reduce | flops 2048 | bytes 16384 | tf_op jit(solution)/shard_map/psum | solution.py:223
  (133 shorter events, 25.5 us)
Async XLA Ops:
  7.2 0.7 copy-start
  7.2 30.5 %copy-start.4 = (bf16[512,1024]{1,0:T(8,128)(2,1)S(1)}, bf16[512,1024]{1,0:T(8,128)(2,1)}, u32[]{:S(2)}) copy-start(bf16[512,1024]{1,0:T(8,128)(2,1)} %param.6) | copy-start | bytes 3145732
  7.2 149.4 %all-gather.16.cloned.1.call-start = ((), (), s32[]{:S(2)}) async-start(), calls=%async_computation.3 | async-start | bytes 1179648 | tf_op jit(solution)/shard_map/all_gather | solution.py:106
  9.0 28.6 %copy-start.6 = (f32[16,512]{1,0:T(8,128)}, f32[16,512]{1,0:T(8,128)S(1)}, u32[]{:S(2)}) copy-start(f32[16,512]{1,0:T(8,128)S(1)} %get-tuple-element.15) | copy-start | bytes 98308
  11.1 272.2 %all-gather.14.cloned.1.call-start = ((), (), s32[]{:S(2)}) async-start(), calls=%async_computation.1 | async-start | bytes 18874368 | tf_op jit(solution)/shard_map/all_gather | solution.py:149
  11.9 345.5 %reduce-scatter.2.cloned.1.call-start = ((), (), s32[]{:S(2)}) async-start(), calls=%async_computation.2 | async-start | bytes 5242880 | tf_op jit(solution)/shard_map/reduce_scatter | solution.py:160
  14.0 134.1 %collective-permute-start = (bf16[2,64,128]{2,1,0:T(8,128)(2,1)}, bf16[2,64,128]{2,1,0:T(8,128)(2,1)}, u32[]{:S(2)}, u32[]{:S(2)}) collective-permute-start(bf16[2,64,128]{2,1,0:T(8,128)(2,1)} %pad_maximum_fusion.2), channel_id=1, source_target_pairs={{0,4},{4,8},{8,12},{12,16},{16,20},{20,24},{24,28},{1,5},{5,9},{9,... | collective-permute-start | bytes 98312 | tf_op jit(solution)/shard_map/ppermute | solution.py:17
  37.7 1.0 copy-start.22
  38.7 2.0 copy-start.2
  40.8 8.4 %copy-start.29 = (u32[32]{0:T(128)S(1)}, u32[32]{0:T(128)}, u32[]{:S(2)}) copy-start(u32[32]{0:T(128)} %constant.94) | copy-start | bytes 388
  47.9 26.8 %copy-start.5 = (bf16[512,128]{1,0:T(8,128)(2,1)S(1)}, bf16[512,128]{1,0:T(8,128)(2,1)}, u32[]{:S(2)}) copy-start(bf16[512,128]{1,0:T(8,128)(2,1)} %param.8) | copy-start | bytes 393220
  70.0 56.3 %copy-start.24 = (f32[16]{0:T(128)}, f32[16]{0:T(128)S(1)}, u32[]{:S(2)}) copy-start(f32[16]{0:T(128)S(1)} %select_reduce_fusion.5) | copy-start | bytes 196
  126.4 14.6 %copy-start.18 = (pred[512,512]{0,1:T(8,128)(4,1)}, pred[512,512]{0,1:T(8,128)(4,1)S(1)}, u32[]{:S(2)}) copy-start(pred[512,512]{0,1:T(8,128)(4,1)S(1)} %iota_compare_fusion) | copy-start | bytes 786436
  126.4 9.5 %copy-start.20 = (f32[1,512,8]{1,2,0:T(8,128)S(1)}, f32[1,512,8]{1,2,0:T(8,128)}, u32[]{:S(2)}) copy-start(f32[1,512,8]{1,2,0:T(8,128)} %copy.68) | copy-start | bytes 49156
  126.4 9.5 %copy-start.21 = (f32[1,512,8]{1,2,0:T(8,128)S(1)}, f32[1,512,8]{1,2,0:T(8,128)}, u32[]{:S(2)}) copy-start(f32[1,512,8]{1,2,0:T(8,128)} %copy.69) | copy-start | bytes 49156
  135.9 11.3 %copy-start.30 = (f32[512,512,8]{1,0,2:T(8,128)}, f32[512,512,8]{1,0,2:T(8,128)S(1)}, u32[]{:S(2)}) copy-start(f32[512,512,8]{1,0,2:T(8,128)S(1)} %get-tuple-element.13) | copy-start | bytes 25165828
  141.0 7.9 %copy-start.8 = (bf16[512,128]{1,0:T(8,128)(2,1)S(1)}, bf16[512,128]{1,0:T(8,128)(2,1)}, u32[]{:S(2)}) copy-start(bf16[512,128]{1,0:T(8,128)(2,1)} %param.7) | copy-start | bytes 393220
  153.6 4.4 copy-start.26
  158.0 8.3 %copy-start.13 = (f32[256,128]{1,0:T(8,128)}, f32[256,128]{1,0:T(8,128)S(1)}, u32[]{:S(2)}) copy-start(f32[256,128]{1,0:T(8,128)S(1)} %select_reduce_fusion.1) | copy-start | bytes 393220
  166.3 14.2 %collective-permute-start.1 = (bf16[512,1024]{0,1:T(8,128)(2,1)S(1)}, bf16[512,1024]{0,1:T(8,128)(2,1)S(1)}, u32[]{:S(2)}, u32[]{:S(2)}) collective-permute-start(bf16[512,1024]{0,1:T(8,128)(2,1)S(1)} %bitcast.373), channel_id=1, source_target_pairs={{0,1},{1,2},{2,3},{3,0},{4,5},{5,6},{6,7},{7,4},{8,9},{9,10},{10,1... | collective-permute-start | bytes 3145736 | tf_op jit(solution)/shard_map/ppermute | solution.py:143
  180.5 14.3 %collective-permute-start.2 = (bf16[512,1024]{0,1:T(8,128)(2,1)S(1)}, bf16[512,1024]{0,1:T(8,128)(2,1)}, u32[]{:S(2)}, u32[]{:S(2)}) collective-permute-start(bf16[512,1024]{0,1:T(8,128)(2,1)S(1)} %collective-permute-done.1), channel_id=1, source_target_pairs={{0,1},{1,2},{2,3},{3,0},{4,5},{5,6},{6,7},{7,4},{8,9},{9,10},{10,1... | collective-permute-start | bytes 3145736 | tf_op jit(solution)/shard_map/ppermute | solution.py:143
  194.8 14.5 %collective-permute-start.3 = (bf16[512,1024]{0,1:T(8,128)(2,1)}, bf16[512,1024]{0,1:T(8,128)(2,1)}, u32[]{:S(2)}, u32[]{:S(2)}) collective-permute-start(bf16[512,1024]{0,1:T(8,128)(2,1)} %collective-permute-done.2), channel_id=1, source_target_pairs={{0,1},{1,2},{2,3},{3,0},{4,5},{5,6},{6,7},{7,4},{8,9},{9,10},{10,1... | collective-permute-start | bytes 3145736 | tf_op jit(solution)/shard_map/ppermute | solution.py:143
  222.8 77.1 %copy-start.27 = (bf16[512,2048]{1,0:T(8,128)(2,1)S(1)}, bf16[512,2048]{1,0:T(8,128)(2,1)}, u32[]{:S(2)}) copy-start(bf16[512,2048]{1,0:T(8,128)(2,1)} %param.11) | copy-start | bytes 6291460
  298.6 1.3 copy-start.28
  313.7 0.7 copy-start.15
  313.8 158.3 %all-gather.18.cloned.1.call-start = ((), (), s32[]{:S(2)}) async-start(), calls=%async_computation.4 | async-start | bytes 1179648 | tf_op jit(solution)/shard_map/all_gather | solution.py:199
  358.8 3.0 copy-start.3
  358.8 6.8 %copy-start.10 = (bf16[512,1024]{1,0:T(8,128)(2,1)S(1)}, bf16[512,1024]{1,0:T(8,128)(2,1)}, u32[]{:S(2)}) copy-start(bf16[512,1024]{1,0:T(8,128)(2,1)} %reduce-scatter.2.cloned.1.call-done) | copy-start | bytes 3145732
  358.8 6.8 %copy-start.16 = (f32[512,1,8]{0,2,1:T(8,128)S(1)}, f32[512,1,8]{0,2,1:T(8,128)}, u32[]{:S(2)}) copy-start(f32[512,1,8]{0,2,1:T(8,128)} %fusion.81) | copy-start | bytes 49156
  365.6 24.9 %copy-start.11 = (bf16[512,1024]{1,0:T(8,128)(2,1)S(1)}, bf16[512,1024]{1,0:T(8,128)(2,1)}, u32[]{:S(2)}) copy-start(bf16[512,1024]{1,0:T(8,128)(2,1)} %reduce-scatter.2.cloned.1.call-done) | copy-start | bytes 3145732
  365.6 24.9 %copy-start.17 = (f32[512,1,8]{0,2,1:T(8,128)S(1)}, f32[512,1,8]{0,2,1:T(8,128)}, u32[]{:S(2)}) copy-start(f32[512,1,8]{0,2,1:T(8,128)} %fusion.81) | copy-start | bytes 49156
  369.9 70.7 %copy-start.12 = (f32[512,8]{1,0:T(8,128)S(1)}, f32[512,8]{1,0:T(8,128)}, u32[]{:S(2)}) copy-start(f32[512,8]{1,0:T(8,128)} %copy.98) | copy-start | bytes 49156
  390.5 50.6 %copy-start.14 = (f32[256,128]{1,0:T(8,128)S(1)}, f32[256,128]{1,0:T(8,128)}, u32[]{:S(2)}) copy-start(f32[256,128]{1,0:T(8,128)} %copy-done.13) | copy-start | bytes 393220
  390.5 50.6 %copy-start.23 = (f32[256]{0:T(256)S(1)}, f32[256]{0:T(256)}, u32[]{:S(2)}) copy-start(f32[256]{0:T(256)} %copy-done.22) | copy-start | bytes 3076
  445.3 1.9 copy-start.25
  445.3 4.1 slice-start
  446.1 3.4 slice-start.1
  447.2 2.2 copy-start.19
  449.5 10.8 %copy-start.7 = (f32[16,512]{1,0:T(8,128)S(1)}, f32[16,512]{1,0:T(8,128)}, u32[]{:S(2)}) copy-start(f32[16,512]{1,0:T(8,128)} %copy-done.6) | copy-start | bytes 98308
  464.3 30.0 %copy-start.1 = (bf16[1,128,16]{1,2,0:T(8,128)(2,1)S(1)}, bf16[1,128,16]{1,2,0:T(8,128)(2,1)}, u32[]{:S(2)}) copy-start(bf16[1,128,16]{1,2,0:T(8,128)(2,1)} %param.9) | copy-start | bytes 12292
  465.0 9.2 %copy-start.9 = (bf16[512,128]{1,0:T(8,128)(2,1)S(1)}, bf16[512,128]{1,0:T(8,128)(2,1)}, u32[]{:S(2)}) copy-start(bf16[512,128]{1,0:T(8,128)(2,1)} %param.7) | copy-start | bytes 393220
Sparse Core Ops, SparseCore 0:
  11.2 42.9 all-gather.15
  56.4 226.8 all-gather.13
  313.9 43.3 reduce-scatter.1
  370.0 40.2 all-gather.17
